TPU v7x, 32 devices: a whole 2x2x4 slice. The times are simulated.
32 devices in a mesh: half: 1, grp: 4 (over y, core), dev: 8 (over z, x).
Axes of the slice: x: 2, y: 2, z: 4, core: 2. Of those that a mesh axis runs over, the one named last changes fastest.
Arguments:
- panel_block: float32 [2048, 512], P(('half', 'grp', 'dev')), may hold values from -1 to 1, as said below
- trailing: float32 [2048, 1024], P(('half', 'grp'), 'dev'), may hold values from -6 to 6
Outputs:
- triangle: float32 [512, 512], replicated
- projected: float32 [512, 1024], P(None, 'dev')
- remainder: float32 [2048, 1024], P(('half', 'grp'), 'dev')
Inputs may be any that keep to these rules, and one draw needn't show every extreme that they name: `panel_block`: of full column rank.
All inputs are finite; a program needn't handle non-finite values.
Results may differ from a plain program's by a relative error of at most 0.0003.
Values sent between devices are 32-bit elements; how exact they have to be, the bound alone decides.
A program may use at most 64 MiB of HBM per device.

v0:
```python
import jax
import jax.numpy as jnp
from jax import lax
from jax.sharding import PartitionSpec as P


def on_device(panel_block, trailing):
    highest = lax.Precision.HIGHEST
    panel_group = lax.all_gather(panel_block, "dev", axis=0, tiled=True)
    gram_part = jnp.dot(panel_group.T, panel_group, precision=highest)
    cross_part = jnp.dot(panel_group.T, trailing, precision=highest)
    gram_sum, cross_sum = lax.psum((gram_part, cross_part), ("half", "grp"))
    factor = jnp.linalg.cholesky(gram_sum)
    projected = lax.linalg.triangular_solve(factor, cross_sum, left_side=True, lower=True)
    solved = lax.linalg.triangular_solve(
        factor, projected, left_side=True, lower=True, transpose_a=True
    )
    remainder = trailing - jnp.dot(panel_group, solved, precision=highest)
    triangle = factor.T
    return (triangle, projected, remainder)


def solution(mesh):
    placed = (P(("half", "grp", "dev"), None), P(("half", "grp"), "dev"))
    return jax.shard_map(
        on_device,
        mesh=mesh,
        in_specs=placed,
        out_specs=(P(), P(None, "dev"), P(("half", "grp"), "dev")),
        check_vma=False,
    )
```

profile of v0, /device:TPU:0, one launch (start us, length us, event | category | flops | bytes accessed | tf_op | source)
XLA Modules:
  0.0 260.0 jit_solution(11239562665385252636)
XLA Ops:
  7.2 0.0 all-gather.2.cloned.1.call-start
  7.2 0.7 all-gather.2.cloned.1.call-update
  7.9 0.0 all-reduce.4.cloned.1.call-start
  8.0 45.2 %all-gather.2.cloned.1.call-done = f32[512,512]{1,0:T(8,128)} async-done(((f32[64,512]{1,0:T(8,128)}), f32[512,512]{1,0:T(8,128)}) %all-gather.2.cloned.1.call-update) | async-done | bytes 1048592 | tf_op jit(solution)/shard_map/all_gather | solution.py:9
  53.1 4.5 %fusion.59 = f32[512,512]{0,1:T(8,128)} fusion(f32[512,512]{1,0:T(8,128)} %all-gather.2.cloned.1.call-done), kind=kOutput, calls=%fused_computation.99 | convolution fusion | flops 1610612736 | bytes 2097152 | tf_op jit(solution)/shard_map/dot_general | solution.py:10
  57.6 2.5 fusion.60
  60.2 0.1 copy.7
  60.3 37.8 %all-reduce.4.cloned.1.call-done = (f32[512,512]{0,1:T(8,128)}, f32[512,128]{1,0:T(8,128)}) async-done(((f32[512,512]{0,1:T(8,128)}, f32[512,128]{1,0:T(8,128)}), (f32[512,512]{0,1:T(8,128)}, f32[512,128]{1,0:T(8,128)})) %all-reduce.4.cloned.1.call-update) | async-done | bytes 1310736 | tf_op jit(solution)/shard_map/psum | solution.py:12
  98.2 1.6 copy.6
  99.8 0.2 fusion.1
  100.1 1.0 copy-done.3
  101.0 11.7 %cholesky.104 = f32[128,128]{1,0:T(8,128)S(1)} custom-call(f32[128,128]{1,0:T(8,128)S(1)} %cholesky.266), custom_call_target="Cholesky" | custom-call | tf_op jit(solution)/shard_map/jit(cholesky)/cholesky | solution.py:13
  112.8 9.8 %custom-call.32 = f32[1,128,128]{1,2,0:T(8,128)S(1)} custom-call(f32[1,128,128]{2,1,0:T(8,128)S(1)} %get-tuple-element.37), custom_call_target="InvertDiagBlocksLowerTriangular" | custom-call | tf_op jit(solution)/shard_map/jit(cholesky)/cholesky | solution.py:13
  122.6 0.1 cholesky.224
  122.7 0.3 constant_dynamic-update-slice_fusion.3
  123.1 0.3 convolution_subtract_fusion
  123.4 0.7 copy-done.6
  124.1 11.9 %cholesky.217 = f32[128,128]{1,0:T(8,128)S(1)} custom-call(f32[128,128]{1,0:T(8,128)S(1)} %cholesky.270), custom_call_target="Cholesky" | custom-call | tf_op jit(solution)/shard_map/jit(cholesky)/cholesky | solution.py:13
  136.0 9.8 %custom-call.33 = f32[1,128,128]{1,2,0:T(8,128)S(1)} custom-call(f32[1,128,128]{2,1,0:T(8,128)S(1)} %get-tuple-element.34), custom_call_target="InvertDiagBlocksLowerTriangular" | custom-call | tf_op jit(solution)/shard_map/jit(cholesky)/cholesky | solution.py:13
  145.8 1.2 convolution_dynamic-update-slice_fusion
  147.0 0.4 convolution_subtract_fusion.1
  147.4 0.6 cholesky.275
  148.0 13.2 %cholesky.238 = f32[128,128]{1,0:T(8,128)} custom-call(f32[128,128]{1,0:T(8,128)} %cholesky.275), custom_call_target="Cholesky" | custom-call | tf_op jit(solution)/shard_map/jit(cholesky)/cholesky | solution.py:13
  161.2 1.5 select_reduce_fusion.1
  162.7 0.7 compare_reduce_fusion.1
  163.4 11.3 %custom-call.34 = f32[1,128,128]{1,2,0:T(8,128)} custom-call(f32[1,128,128]{2,1,0:T(8,128)} %get-tuple-element.31), custom_call_target="InvertDiagBlocksLowerTriangular" | custom-call | tf_op jit(solution)/shard_map/jit(cholesky)/cholesky | solution.py:13
  174.7 1.0 convolution_dynamic-update-slice_fusion.1
  175.7 0.4 convolution_subtract_fusion.8
  176.1 11.9 %cholesky.255 = f32[128,128]{1,0:T(8,128)S(1)} custom-call(f32[128,128]{1,0:T(8,128)S(1)} %convolution_subtract_fusion.8), custom_call_target="Cholesky" | custom-call | tf_op jit(solution)/shard_map/jit(cholesky)/cholesky | solution.py:13
  188.0 0.6 compare_reduce_fusion
  188.6 0.6 compare_reduce_fusion.2
  191.8 1.2 fusion.2
  193.1 10.9 %while.1 = (s32[]{:T(128)}, f32[512,512]{1,0:T(8,128)S(1)}, s32[4,2]{0,1:T(2,128)S(1)}, f32[4,128,128]{2,1,0:T(8,128)}, s32[]{:T(128)}) while((s32[]{:T(128)}, f32[512,512]{1,0:T(8,128)S(1)}, s32[4,2]{0,1:T(2,128)S(1)}, f32[4,128,128]{2,1,0:T(8,128)}, s32[]{:T(128)}) %tuple.33), condition=%wide.while_cond, body=%wide.while_body.sunk | while | flops 2 | bytes 132705 | solution.py:14
  193.1 0.1 constant_dynamic-slice_fusion.2
  193.1 0.6 fusion.77
  193.7 2.1 bitcast_dynamic-update-slice_fusion.2
  195.8 0.1 constant_dynamic-slice_fusion.2
  195.9 0.6 fusion.77
  196.5 2.1 bitcast_dynamic-update-slice_fusion.2
  198.5 0.1 constant_dynamic-slice_fusion.2
  198.6 0.6 fusion.77
  199.2 2.1 bitcast_dynamic-update-slice_fusion.2
  201.3 0.1 constant_dynamic-slice_fusion.2
  201.3 0.6 fusion.77
  201.9 2.1 bitcast_dynamic-update-slice_fusion.2
  204.0 40.1 %custom-call.35 = f32[4,128,128]{1,2,0:T(8,128)S(1)} custom-call(f32[4,128,128]{2,1,0:T(8,128)} %get-tuple-element.10), custom_call_target="InvertDiagBlocksLowerTriangular" | custom-call | tf_op jit(solution)/shard_map/triangular_solve | solution.py:14
  244.1 1.1 fusion.39
  245.3 0.2 convolution_subtract_fusion.5
  245.5 0.3 fusion.48
  245.8 0.3 convolution_subtract_fusion.4
  246.0 0.3 fusion.50
  246.3 0.3 convolution_subtract_fusion.7
  246.7 0.3 fusion.52
  246.9 0.2 fusion.51
  247.2 0.7 pad_maximum_fusion
  247.9 0.3 convolution_subtract_fusion.3
  248.2 0.2 fusion.49
  248.4 0.4 convolution_subtract_fusion.2
  248.8 0.2 fusion.47
  249.0 0.5 convolution_subtract_fusion.6
  249.5 0.2 fusion.46
  249.7 1.3 fusion
  251.0 0.8 copy.9
  251.8 1.3 copy.8
  (23 shorter events, 0.2 us)
Async XLA Ops:
  7.2 46.0 %all-gather.2.cloned.1.call-start = ((), (), s32[]{:S(2)}) async-start(), calls=%async_computation | async-start | bytes 1179648 | tf_op jit(solution)/shard_map/all_gather | solution.py:9
  7.9 49.7 %copy-start.5 = (f32[512,128]{1,0:T(8,128)S(1)}, f32[512,128]{1,0:T(8,128)}, u32[]{:S(2)}) copy-start(f32[512,128]{1,0:T(8,128)} %param.3) | copy-start | bytes 786436
  7.9 90.2 %all-reduce.4.cloned.1.call-start = ((), (), s32[]{:S(2)}) async-start(), calls=%async_computation.1 | async-start | bytes 2621440 | tf_op jit(solution)/shard_map/psum | solution.py:12
  53.1 4.5 %copy-start = (f32[512,512]{1,0:T(8,128)S(1)}, f32[512,512]{1,0:T(8,128)}, u32[]{:S(2)}) copy-start(f32[512,512]{1,0:T(8,128)} %all-gather.2.cloned.1.call-done) | copy-start | bytes 3145732
  98.2 1.7 copy-start.1
  100.0 1.0 copy-start.3
  101.0 21.7 %copy-start.4 = (f32[512,512]{1,0:T(8,128)S(1)}, f32[512,512]{1,0:T(8,128)}, u32[]{:S(2)}) copy-start(f32[512,512]{1,0:T(8,128)} %copy-done.3) | copy-start | bytes 3145732
  123.4 0.7 copy-start.6
  193.1 52.2 %copy-start.7 = (f32[512,128]{1,0:T(8,128)S(1)}, f32[512,128]{1,0:T(8,128)}, u32[]{:S(2)}) copy-start(f32[512,128]{1,0:T(8,128)} %get-tuple-element.23) | copy-start | bytes 786436
  249.7 2.1 copy-start.2
Sparse Core Ops, SparseCore 0:
  10.1 42.9 all-gather.1
  60.3 37.8 all-reduce.3
where the time goes:
time: 261 us; the launch traced here: 260 us
  other arithmetic  125 us (48%)
  waiting for transfers between devices  83.7 us (32%)
  local copies, waits for them, and re-layouts  17.3 us (7%)
  between operations  16.9 us (6%)
  matrix products  16.6 us (6%)
    another operation x14, other arithmetic, on_device(): factor = jnp.linalg.cholesky(gram_sum)  83.1 us
    all_gather x1, waiting for transfers between devices, on_device(): panel_group = lax.all_gather(panel_block, 'dev', axis=0, tiled=True)  45.2 us
    another operation x4, other arithmetic, on_device(): lax.linalg.triangular_solve(factor, cross_sum, left_side=True, lower=True)  42.1 us
    psum x1, waiting for transfers between devices, on_device(): gram_sum, cross_sum = lax.psum((gram_part, cross_part), ('half', 'grp'))  37.8 us
    another operation x12, local copies, waits for them, and re-layouts  10.9 us
  transfers between devices with their start and end apart: 2, of which 2 were waited for; matrix products, arithmetic and copies ran while one was open for 0% of the time, Pallas kernels for 0%

commit v1 on v0

--- a/solution.py
+++ b/solution.py
@@ -6,7 +6,12 @@
 
 def on_device(panel_block, trailing):
     highest = lax.Precision.HIGHEST
-    panel_group = lax.all_gather(panel_block, "dev", axis=0, tiled=True)
+    ring = [panel_block]
+    for hop in range(7):
+        ring.append(lax.ppermute(ring[-1], "dev", [(dev, (dev + 1) % 8) for dev in range(8)]))
+    panel_group = jnp.roll(
+        jnp.concatenate(ring[::-1], axis=0), (lax.axis_index("dev") + 1) * ring[0].shape[0], axis=0
+    )
     gram_part = jnp.dot(panel_group.T, panel_group, precision=highest)
     cross_part = jnp.dot(panel_group.T, trailing, precision=highest)
     gram_sum, cross_sum = lax.psum((gram_part, cross_part), ("half", "grp"))

time: 261 us -> 276 us (1.057)
  waiting for transfers between devices: 83.7 us -> 90.9 us
  matrix products: 16.6 us -> 21.8 us
  other arithmetic: 125 us -> 122 us
  starting transfers between devices: 0.08 us -> 3.07 us
    ppermute x0 -> x7, waiting for transfers between devices: none -> 54 us  [on_device(): lax.ppermute(ring[-1], 'dev', [(dev, (dev + 1) % 8) for dev in range(8)])]
    all_gather x1 -> x0, waiting for transfers between devices: 45.2 us -> none  [on_device(): panel_group = lax.all_gather(panel_block, 'dev', axis=0, tiled=True)]
    another operation x14, other arithmetic: 83.1 us -> 78.6 us  [on_device(): factor = jnp.linalg.cholesky(gram_sum)]
    ppermute x0 -> x7, starting transfers between devices: none -> 3.04 us  [on_device(): lax.ppermute(ring[-1], 'dev', [(dev, (dev + 1) % 8) for dev in range(8)])]
    another operation x12, local copies, waits for them, and re-layouts: 10.9 us -> 13.7 us
  transfers between devices with their start and end apart: 2 -> 8, of which waited for: 2 -> 8; matrix products, arithmetic and copies ran while one was open for 0% -> 0% of each run, Pallas kernels for 0% -> 0%
where the time goes in v1:
time: 276 us; the launch traced here: 275 us
  other arithmetic  122 us (44%)
  waiting for transfers between devices  90.9 us (33%)
  matrix products  21.8 us (8%)
  local copies, waits for them, and re-layouts  19.9 us (7%)
  between operations  17.2 us (6%)
  starting transfers between devices  3.07 us (1%)
    another operation x14, other arithmetic, on_device(): factor = jnp.linalg.cholesky(gram_sum)  78.6 us
    ppermute x7, waiting for transfers between devices, on_device(): lax.ppermute(ring[-1], 'dev', [(dev, (dev + 1) % 8) for dev in range(8)])  54 us
    another operation x4, other arithmetic, on_device(): lax.linalg.triangular_solve(factor, cross_sum, left_side=True, lower=True)  42.4 us
    psum x1, waiting for transfers between devices, on_device(): gram_sum, cross_sum = lax.psum((gram_part, cross_part), ('half', 'grp'))  36.9 us
    another operation x12, local copies, waits for them, and re-layouts  13.7 us
  transfers between devices with their start and end apart: 8, of which 8 were waited for; matrix products, arithmetic and copies ran while one was open for 0% of the time, Pallas kernels for 0%

profile of v1, /device:TPU:0, one launch (start us, length us, event | category | flops | bytes accessed | tf_op | source)
XLA Modules:
  0.0 275.4 jit_solution(13586894433757514804)
XLA Ops:
  7.2 3.0 %collective-permute-start = (f32[64,512]{1,0:T(8,128)}, f32[64,512]{1,0:T(8,128)S(1)}, u32[]{:S(2)}, u32[]{:S(2)}) collective-permute-start(f32[64,512]{1,0:T(8,128)} %param.2), channel_id=1, source_target_pairs={{0,1},{1,2},{2,3},{3,4},{4,5},{5,6},{6,7},{7,0},{8,9},{9,10},{10,1... | collective-permute-start | bytes 393224 | tf_op jit(solution)/shard_map/ppermute | solution.py:11
  10.2 6.7 %collective-permute-done = f32[64,512]{1,0:T(8,128)S(1)} collective-permute-done((f32[64,512]{1,0:T(8,128)}, f32[64,512]{1,0:T(8,128)S(1)}, u32[]{:S(2)}, u32[]{:S(2)}) %collective-permute-start) | collective-permute-done | bytes 131104 | tf_op jit(solution)/shard_map/ppermute | solution.py:11
  17.0 7.7 %collective-permute-done.1 = f32[64,512]{1,0:T(8,128)S(1)} collective-permute-done((f32[64,512]{1,0:T(8,128)S(1)}, f32[64,512]{1,0:T(8,128)S(1)}, u32[]{:S(2)}, u32[]{:S(2)}) %collective-permute-start.1) | collective-permute-done | bytes 131104 | tf_op jit(solution)/shard_map/ppermute | solution.py:11
  24.7 7.7 %collective-permute-done.2 = f32[64,512]{1,0:T(8,128)S(1)} collective-permute-done((f32[64,512]{1,0:T(8,128)S(1)}, f32[64,512]{1,0:T(8,128)S(1)}, u32[]{:S(2)}, u32[]{:S(2)}) %collective-permute-start.2) | collective-permute-done | bytes 131104 | tf_op jit(solution)/shard_map/ppermute | solution.py:11
  32.3 7.7 %collective-permute-done.3 = f32[64,512]{1,0:T(8,128)S(1)} collective-permute-done((f32[64,512]{1,0:T(8,128)S(1)}, f32[64,512]{1,0:T(8,128)S(1)}, u32[]{:S(2)}, u32[]{:S(2)}) %collective-permute-start.3) | collective-permute-done | bytes 131104 | tf_op jit(solution)/shard_map/ppermute | solution.py:11
  40.0 7.7 %collective-permute-done.4 = f32[64,512]{1,0:T(8,128)S(1)} collective-permute-done((f32[64,512]{1,0:T(8,128)S(1)}, f32[64,512]{1,0:T(8,128)S(1)}, u32[]{:S(2)}, u32[]{:S(2)}) %collective-permute-start.4) | collective-permute-done | bytes 131104 | tf_op jit(solution)/shard_map/ppermute | solution.py:11
  47.7 8.9 %collective-permute-done.5 = f32[64,512]{1,0:T(8,128)S(1)} collective-permute-done((f32[64,512]{1,0:T(8,128)S(1)}, f32[64,512]{1,0:T(8,128)S(1)}, u32[]{:S(2)}, u32[]{:S(2)}) %collective-permute-start.5) | collective-permute-done | bytes 131104 | tf_op jit(solution)/shard_map/ppermute | solution.py:11
  56.6 7.7 %collective-permute-done.6 = f32[64,512]{1,0:T(8,128)S(1)} collective-permute-done((f32[64,512]{1,0:T(8,128)S(1)}, f32[64,512]{1,0:T(8,128)S(1)}, u32[]{:S(2)}, u32[]{:S(2)}) %collective-permute-start.6) | collective-permute-done | bytes 131104 | tf_op jit(solution)/shard_map/ppermute | solution.py:11
  64.3 0.9 constant_dynamic-update-slice_fusion.8
  65.4 2.9 %fusion.5 = f32[512,512]{0,1:T(8,128)} fusion(f32[1024,512]{1,0:T(8,128)S(1)} %constant_dynamic-update-slice_fusion, s32[]{:T(128)S(6)} %select_n.18), kind=kOutput, calls=%fused_computation.22 | convolution fusion | flops 1610612736 | bytes 2097156 | tf_op jit(solution)/shard_map/dot_general | solution.py:15
  68.3 2.5 fusion.3
  70.9 36.9 %all-reduce.4.cloned.1.call-done = (f32[512,512]{0,1:T(8,128)}, f32[512,128]{1,0:T(8,128)}) async-done(((f32[512,512]{0,1:T(8,128)}, f32[512,128]{1,0:T(8,128)}), (f32[512,512]{0,1:T(8,128)}, f32[512,128]{1,0:T(8,128)})) %all-reduce.4.cloned.1.call-update) | async-done | bytes 1310736 | tf_op jit(solution)/shard_map/psum | solution.py:17
  107.8 2.6 copy.6
  110.4 1.4 fusion
  111.9 1.0 copy-done.2
  112.8 11.7 %cholesky.104 = f32[128,128]{1,0:T(8,128)S(1)} custom-call(f32[128,128]{1,0:T(8,128)S(1)} %cholesky.266), custom_call_target="Cholesky" | custom-call | tf_op jit(solution)/shard_map/jit(cholesky)/cholesky | solution.py:18
  124.6 0.1 cholesky.224
  124.7 9.8 %custom-call.32 = f32[1,128,128]{1,2,0:T(8,128)S(1)} custom-call(f32[1,128,128]{2,1,0:T(8,128)S(1)} %get-tuple-element.37), custom_call_target="InvertDiagBlocksLowerTriangular" | custom-call | tf_op jit(solution)/shard_map/jit(cholesky)/cholesky | solution.py:18
  134.5 1.2 constant_dynamic-update-slice_fusion.19
  135.8 1.3 convolution_subtract_fusion.1
  137.1 11.9 %cholesky.217 = f32[128,128]{1,0:T(8,128)S(1)} custom-call(f32[128,128]{1,0:T(8,128)S(1)} %cholesky.270), custom_call_target="Cholesky" | custom-call | tf_op jit(solution)/shard_map/jit(cholesky)/cholesky | solution.py:18
  149.0 9.8 %custom-call.33 = f32[1,128,128]{1,2,0:T(8,128)S(1)} custom-call(f32[1,128,128]{2,1,0:T(8,128)S(1)} %get-tuple-element.34), custom_call_target="InvertDiagBlocksLowerTriangular" | custom-call | tf_op jit(solution)/shard_map/jit(cholesky)/cholesky | solution.py:18
  158.8 0.3 convolution_dynamic-update-slice_fusion
  159.0 1.3 convolution_subtract_fusion.2
  160.3 11.7 %cholesky.238 = f32[128,128]{1,0:T(8,128)S(1)} custom-call(f32[128,128]{1,0:T(8,128)S(1)} %cholesky.275), custom_call_target="Cholesky" | custom-call | tf_op jit(solution)/shard_map/jit(cholesky)/cholesky | solution.py:18
  172.1 0.7 compare_reduce_fusion.1
  172.8 9.8 %custom-call.34 = f32[1,128,128]{1,2,0:T(8,128)S(1)} custom-call(f32[1,128,128]{2,1,0:T(8,128)S(1)} %get-tuple-element.31), custom_call_target="InvertDiagBlocksLowerTriangular" | custom-call | tf_op jit(solution)/shard_map/jit(cholesky)/cholesky | solution.py:18
  182.6 0.2 convolution_dynamic-update-slice_fusion.1
  182.8 1.2 convolution_subtract_fusion.9
  184.2 11.7 %cholesky.255 = f32[128,128]{1,0:T(8,128)S(1)} custom-call(f32[128,128]{1,0:T(8,128)S(1)} %convolution_subtract_fusion.9), custom_call_target="Cholesky" | custom-call | tf_op jit(solution)/shard_map/jit(cholesky)/cholesky | solution.py:18
  196.0 0.7 compare_reduce_fusion
  196.7 0.6 compare_reduce_fusion.2
  199.9 1.6 fusion.1
  201.5 13.7 %while.1 = (s32[]{:T(128)}, f32[512,512]{1,0:T(8,128)}, s32[4,2]{0,1:T(2,128)S(1)}, f32[4,128,128]{2,1,0:T(8,128)}, s32[]{:T(128)}) while((s32[]{:T(128)}, f32[512,512]{1,0:T(8,128)}, s32[4,2]{0,1:T(2,128)S(1)}, f32[4,128,128]{2,1,0:T(8,128)}, s32[]{:T(128)}) %tuple.33), condition=%wide.while_cond, body=%wide.while_body.sunk | while | flops 2 | bytes 132705 | solution.py:19
  201.5 0.1 constant_dynamic-slice_fusion.2
  201.6 0.5 fusion.78
  202.1 2.9 %bitcast_dynamic-update-slice_fusion.2 = f32[4,128,128]{2,1,0:T(8,128)} fusion(f32[4,128,128]{2,1,0:T(8,128)} %get-tuple-element.79, s32[]{:T(128)} %get-tuple-element.76, f32[512,512]{1,0:T(8,128)} %get-tuple-element.82, s32[]{:T(128)} %bitcast.58, s32[]{:T(128)} %bitcast.59), kind=kLoop, calls=%fused_computation.clone.1 | loop fusion | bytes 132608 | tf_op jit(solution)/shard_map/triangular_solve
  204.9 0.1 constant_dynamic-slice_fusion.2
  205.0 0.5 fusion.78
  205.5 2.9 %bitcast_dynamic-update-slice_fusion.2 = f32[4,128,128]{2,1,0:T(8,128)} fusion(f32[4,128,128]{2,1,0:T(8,128)} %get-tuple-element.79, s32[]{:T(128)} %get-tuple-element.76, f32[512,512]{1,0:T(8,128)} %get-tuple-element.82, s32[]{:T(128)} %bitcast.58, s32[]{:T(128)} %bitcast.59), kind=kLoop, calls=%fused_computation.clone.1 | loop fusion | bytes 132608 | tf_op jit(solution)/shard_map/triangular_solve
  208.4 0.1 constant_dynamic-slice_fusion.2
  208.5 0.5 fusion.78
  209.0 2.9 %bitcast_dynamic-update-slice_fusion.2 = f32[4,128,128]{2,1,0:T(8,128)} fusion(f32[4,128,128]{2,1,0:T(8,128)} %get-tuple-element.79, s32[]{:T(128)} %get-tuple-element.76, f32[512,512]{1,0:T(8,128)} %get-tuple-element.82, s32[]{:T(128)} %bitcast.58, s32[]{:T(128)} %bitcast.59), kind=kLoop, calls=%fused_computation.clone.1 | loop fusion | bytes 132608 | tf_op jit(solution)/shard_map/triangular_solve
  211.8 0.1 constant_dynamic-slice_fusion.2
  211.9 0.5 fusion.78
  212.4 2.8 %bitcast_dynamic-update-slice_fusion.2 = f32[4,128,128]{2,1,0:T(8,128)} fusion(f32[4,128,128]{2,1,0:T(8,128)} %get-tuple-element.79, s32[]{:T(128)} %get-tuple-element.76, f32[512,512]{1,0:T(8,128)} %get-tuple-element.82, s32[]{:T(128)} %bitcast.58, s32[]{:T(128)} %bitcast.59), kind=kLoop, calls=%fused_computation.clone.1 | loop fusion | bytes 132608 | tf_op jit(solution)/shard_map/triangular_solve
  215.2 40.1 %custom-call.35 = f32[4,128,128]{1,2,0:T(8,128)S(1)} custom-call(f32[4,128,128]{2,1,0:T(8,128)} %get-tuple-element.10), custom_call_target="InvertDiagBlocksLowerTriangular" | custom-call | tf_op jit(solution)/shard_map/triangular_solve | solution.py:19
  255.4 0.3 fusion.43
  255.7 1.1 convolution_subtract_fusion.6
  256.8 0.3 fusion.52
  257.0 1.2 convolution_subtract_fusion.5
  258.2 0.3 fusion.54
  258.5 1.2 convolution_subtract_fusion.8
  259.8 0.3 fusion.56
  260.1 0.2 fusion.55
  260.3 0.7 pad_maximum_fusion
  261.0 1.1 convolution_subtract_fusion.4
  262.1 0.2 fusion.53
  262.4 1.3 convolution_subtract_fusion.3
  263.7 0.2 fusion.51
  263.9 1.4 convolution_subtract_fusion.7
  265.3 0.2 fusion.50
  265.5 1.7 convolution_subtract_fusion
  267.2 1.3 copy.7
  (46 shorter events, 0.5 us)
Async XLA Ops:
  7.2 58.3 %copy-start.5 = (f32[64,512]{1,0:T(8,128)S(1)}, f32[64,512]{1,0:T(8,128)}, u32[]{:S(2)}) copy-start(f32[64,512]{1,0:T(8,128)} %param.2) | copy-start | bytes 393220
  7.2 100.6 %all-reduce.4.cloned.1.call-start = ((), (), s32[]{:S(2)}) async-start(), calls=%async_computation | async-start | bytes 2621440 | tf_op jit(solution)/shard_map/psum | solution.py:17
  7.2 9.8 %collective-permute-start = (f32[64,512]{1,0:T(8,128)}, f32[64,512]{1,0:T(8,128)S(1)}, u32[]{:S(2)}, u32[]{:S(2)}) collective-permute-start(f32[64,512]{1,0:T(8,128)} %param.2), channel_id=1, source_target_pairs={{0,1},{1,2},{2,3},{3,4},{4,5},{5,6},{6,7},{7,0},{8,9},{9,10},{10,1... | collective-permute-start | bytes 393224 | tf_op jit(solution)/shard_map/ppermute | solution.py:11
  17.0 7.7 %collective-permute-start.1 = (f32[64,512]{1,0:T(8,128)S(1)}, f32[64,512]{1,0:T(8,128)S(1)}, u32[]{:S(2)}, u32[]{:S(2)}) collective-permute-start(f32[64,512]{1,0:T(8,128)S(1)} %collective-permute-done), channel_id=1, source_target_pairs={{0,1},{1,2},{2,3},{3,4},{4,5},{5,6},{6,7},{7,0},{8,9},{9,10},{10,1... | collective-permute-start | bytes 393224 | tf_op jit(solution)/shard_map/ppermute | solution.py:11
  24.7 7.7 %collective-permute-start.2 = (f32[64,512]{1,0:T(8,128)S(1)}, f32[64,512]{1,0:T(8,128)S(1)}, u32[]{:S(2)}, u32[]{:S(2)}) collective-permute-start(f32[64,512]{1,0:T(8,128)S(1)} %collective-permute-done.1), channel_id=1, source_target_pairs={{0,1},{1,2},{2,3},{3,4},{4,5},{5,6},{6,7},{7,0},{8,9},{9,10},{10,1... | collective-permute-start | bytes 393224 | tf_op jit(solution)/shard_map/ppermute | solution.py:11
  32.3 7.7 %collective-permute-start.3 = (f32[64,512]{1,0:T(8,128)S(1)}, f32[64,512]{1,0:T(8,128)S(1)}, u32[]{:S(2)}, u32[]{:S(2)}) collective-permute-start(f32[64,512]{1,0:T(8,128)S(1)} %collective-permute-done.2), channel_id=1, source_target_pairs={{0,1},{1,2},{2,3},{3,4},{4,5},{5,6},{6,7},{7,0},{8,9},{9,10},{10,1... | collective-permute-start | bytes 393224 | tf_op jit(solution)/shard_map/ppermute | solution.py:11
  40.0 7.7 %collective-permute-start.4 = (f32[64,512]{1,0:T(8,128)S(1)}, f32[64,512]{1,0:T(8,128)S(1)}, u32[]{:S(2)}, u32[]{:S(2)}) collective-permute-start(f32[64,512]{1,0:T(8,128)S(1)} %collective-permute-done.3), channel_id=1, source_target_pairs={{0,1},{1,2},{2,3},{3,4},{4,5},{5,6},{6,7},{7,0},{8,9},{9,10},{10,1... | collective-permute-start | bytes 393224 | tf_op jit(solution)/shard_map/ppermute | solution.py:11
  47.7 8.9 %collective-permute-start.5 = (f32[64,512]{1,0:T(8,128)S(1)}, f32[64,512]{1,0:T(8,128)S(1)}, u32[]{:S(2)}, u32[]{:S(2)}) collective-permute-start(f32[64,512]{1,0:T(8,128)S(1)} %collective-permute-done.4), channel_id=1, source_target_pairs={{0,1},{1,2},{2,3},{3,4},{4,5},{5,6},{6,7},{7,0},{8,9},{9,10},{10,1... | collective-permute-start | bytes 393224 | tf_op jit(solution)/shard_map/ppermute | solution.py:11
  56.5 7.7 %collective-permute-start.6 = (f32[64,512]{1,0:T(8,128)S(1)}, f32[64,512]{1,0:T(8,128)S(1)}, u32[]{:S(2)}, u32[]{:S(2)}) collective-permute-start(f32[64,512]{1,0:T(8,128)S(1)} %collective-permute-done.5), channel_id=1, source_target_pairs={{0,1},{1,2},{2,3},{3,4},{4,5},{5,6},{6,7},{7,0},{8,9},{9,10},{10,1... | collective-permute-start | bytes 393224 | tf_op jit(solution)/shard_map/ppermute | solution.py:11
  65.3 3.0 %copy-start.3 = (f32[512,128]{1,0:T(8,128)S(1)}, f32[512,128]{1,0:T(8,128)}, u32[]{:S(2)}) copy-start(f32[512,128]{1,0:T(8,128)} %param.3) | copy-start | bytes 786436
  107.8 2.6 copy-start
  111.9 1.0 copy-start.2
  184.2 71.1 %copy-start.6 = (f32[512,128]{1,0:T(8,128)S(1)}, f32[512,128]{1,0:T(8,128)}, u32[]{:S(2)}) copy-start(f32[512,128]{1,0:T(8,128)} %get-tuple-element.23) | copy-start | bytes 786436
  255.6 9.9 %copy-start.4 = (f32[512,128]{1,0:T(8,128)S(1)}, f32[512,128]{1,0:T(8,128)}, u32[]{:S(2)}) copy-start(f32[512,128]{1,0:T(8,128)} %param.3) | copy-start | bytes 786436
  260.3 6.9 %copy-start.1 = (f32[512,512]{0,1:T(8,128)S(1)}, f32[512,512]{0,1:T(8,128)}, u32[]{:S(2)}) copy-start(f32[512,512]{0,1:T(8,128)} %get-tuple-element.27) | copy-start | bytes 3145732
Sparse Core Ops, SparseCore 0:
  71.0 36.7 all-reduce.3
